TPU v7x, 512 devices: a whole 4x8x8 slice. The times are simulated.
512 devices in a mesh: seq: 64 (over x, y, core), head: 8 (over z).
Axes of the slice: x: 4, y: 8, z: 8, core: 2. Of those that a mesh axis runs over, the one named last changes fastest.
Arguments:
- queries: bfloat16 [69632, 2048], P('seq', 'head'), may hold values from -50 to 50
- keys: bfloat16 [69632, 2048], P('seq', 'head'), may hold values from -6 to 6
- values: bfloat16 [69632, 2048], P('seq', 'head'), may hold values from -48 to 48
- rand_group: int32 [1088, 3], replicated, may hold values from 0 to 63, all different within a row; in each aligned block of 17 rows (0 to 16, 17 to 33, ...) at most 2 rows name the same one
- rand_offset: int32 [1088, 3], replicated, may hold values from 0 to 16
- glob_blocks: int32 [2], replicated, may hold values from 0 to 1087
- w_out: bfloat16 [2048, 4096], P(None, 'head'), may hold values from -0.125 to 0.125
Outputs:
- layer_out: bfloat16 [69632, 4096], P('seq', 'head')
Inputs may be any that keep to these rules, and one draw needn't show every extreme that they name: `rand_group`: each row names 3 different groups. Among the 17 rows of one aligned block of 17 rows, no group is named more than 2 times, and in every draw some group is named exactly 2 times in some such block.
All inputs are finite; a program needn't handle non-finite values.
Results may differ from a plain program's by a relative error of at most 0.0056.
Values may be sent and summed in bfloat16 or wider, within the bound.
A program may use at most 128 MiB of HBM per device.

v0:
```python
from functools import reduce
import math

import jax
import jax.numpy as jnp
from jax import lax
from jax.sharding import PartitionSpec as P

DH = 128
BLOCK = 64
R = 3
G = 2


def padded_2(x, sides, width):
    for axis, dim in sides:
        size, length = (lax.axis_size(axis), x.shape[dim])
        up = [(i, (i + 1) % size) for i in range(size)]
        down = [(j, i) for i, j in up]
        last = lax.slice_in_dim(x, length - width, length, axis=dim)
        initial = lax.slice_in_dim(x, 0, width, axis=dim)
        before = lax.ppermute(last, axis, up)
        after = lax.ppermute(initial, axis, down)
        x = jnp.concatenate([before, x, after], axis=dim)
    return x


def spread(block, axis, holder):
    block = jnp.where(lax.axis_index(axis) == holder, block, jnp.zeros_like(block))
    return lax.psum(block, axis)


def attend_sets(query_rows, pair_sets, columns):
    head_count = columns // DH
    block_count = query_rows.shape[0]
    query_heads = query_rows.reshape(block_count, BLOCK, head_count, DH)
    score_scale = 1.0 / math.sqrt(DH)
    score_list = []
    for pair_rows in pair_sets:
        key_part = pair_rows[..., :columns].reshape(block_count, -1, head_count, DH)
        score_list.append(
            jnp.einsum("nqhd,nkhd->nhqk", query_heads, key_part, preferred_element_type=jnp.float32)
            * score_scale
        )
    row_max = reduce(
        jnp.maximum, [jnp.max(score_part, axis=-1, keepdims=True) for score_part in score_list]
    )
    row_total = jnp.zeros((block_count, head_count, BLOCK), jnp.float32)
    weighted = jnp.zeros((block_count, BLOCK, head_count, DH), jnp.float32)
    for score_part, pair_rows in zip(score_list, pair_sets):
        weights = jnp.exp(score_part - row_max)
        row_total = jnp.sum(weights, axis=-1)
        value_part = pair_rows[..., columns:].reshape(block_count, -1, head_count, DH)
        weighted = jnp.einsum(
            "nhqk,nkhd->nqhd",
            weights.astype(jnp.bfloat16),
            value_part,
            preferred_element_type=jnp.float32,
        )
    context = weighted / jnp.transpose(row_total, (0, 2, 1))[..., None]
    return context.astype(jnp.bfloat16).reshape(block_count * BLOCK, columns)


def on_device(queries, keys, values, rand_group, rand_offset, glob_blocks, w_out):
    columns = queries.shape[1]
    tokens_dev = queries.shape[0]
    per_device = tokens_dev // BLOCK
    seq_count = lax.axis_size("seq")
    my_index = lax.axis_index("seq")
    slot_cap = rand_group.shape[0] // seq_count * R
    slot_cap = max(2, (slot_cap + seq_count - 1) // seq_count)
    pair_rows = jnp.concatenate([keys, values], axis=1)
    pair_blocks = pair_rows.reshape(per_device, BLOCK, 2 * columns)
    padded = padded_2(pair_rows, (("seq", 0),), BLOCK)
    padded_blocks = padded.reshape(per_device + 2, BLOCK, 2 * columns)
    window_sets = jnp.stack([padded_blocks[:-2], padded_blocks[1:-1], padded_blocks[2:]], axis=1)
    found = []
    for global_slot in range(G):
        owner_index = glob_blocks[global_slot] // per_device
        local_spot = glob_blocks[global_slot] % per_device
        piece_rows = lax.dynamic_index_in_dim(pair_blocks, local_spot, 0, keepdims=False)
        found.append(spread(piece_rows, "seq", owner_index))
    global_pairs = jnp.stack(found)
    global_sets = jnp.broadcast_to(global_pairs[None], (per_device, G, BLOCK, 2 * columns))
    request_count = per_device * R
    asked_groups = rand_group.reshape(seq_count, request_count)
    asked_offsets = rand_offset.reshape(seq_count, request_count)
    asked_here = (asked_groups == my_index).astype(jnp.int32)
    slot_rank = jnp.cumsum(asked_here, axis=1) - asked_here
    slot_index = jnp.arange(slot_cap, dtype=jnp.int32)
    slot_match = (asked_here[:, None, :] == 1) & (
        slot_rank[:, None, :] == slot_index[None, :, None]
    )
    send_spot = jnp.sum(jnp.where(slot_match, asked_offsets[:, None, :], 0), axis=2)
    slot_filled = jnp.any(slot_match, axis=2)
    outgoing = jnp.take(pair_blocks, send_spot.reshape(-1), axis=0).reshape(
        seq_count, slot_cap, BLOCK, 2 * columns
    )
    outgoing = jnp.where(slot_filled[:, :, None, None], outgoing, jnp.zeros_like(outgoing))
    incoming = lax.all_to_all(outgoing, "seq", split_axis=0, concat_axis=0, tiled=True)
    my_groups = lax.dynamic_slice_in_dim(rand_group, my_index * per_device, per_device, 0).reshape(
        -1
    )
    request_index = jnp.arange(request_count, dtype=jnp.int32)
    earlier_same = (my_groups[None, :] == my_groups[:, None]) & (
        request_index[None, :] < request_index[:, None]
    )
    arrival_rank = jnp.sum(earlier_same.astype(jnp.int32), axis=1)
    arrival_spot = my_groups * slot_cap + arrival_rank
    random_sets = jnp.take(
        incoming.reshape(seq_count * slot_cap, BLOCK, 2 * columns), arrival_spot, axis=0
    )
    random_sets = random_sets.reshape(per_device, R, BLOCK, 2 * columns)
    query_rows = queries.reshape(per_device, BLOCK, columns)
    joined_sets = jnp.concatenate([window_sets, global_sets, random_sets], axis=1).reshape(
        per_device, -1, 2 * columns
    )
    context = attend_sets(query_rows, [joined_sets], columns)
    summed = jnp.dot(
        lax.all_gather(context, "head", axis=1, tiled=True),
        w_out,
        preferred_element_type=jnp.float32,
    )
    return summed.astype(jnp.bfloat16)


def solution(mesh):
    return jax.shard_map(
        on_device,
        mesh=mesh,
        in_specs=(
            P("seq", "head"),
            P("seq", "head"),
            P("seq", "head"),
            P(),
            P(),
            P(),
            P(None, "head"),
        ),
        out_specs=P("seq", "head"),
        check_vma=False,
    )
```

profile of v0, /device:TPU:6, one launch (start us, length us, event | category | flops | bytes accessed | tf_op | source)
XLA Modules:
  0.0 396.3 jit_solution(1737452305502771908)
XLA Ops:
  6.5 0.9 compare_convert_fusion
  7.4 0.2 copy.53
  8.3 1.0 copy.58
  9.8 1.1 constant_dynamic-update-slice_fusion.1
  11.3 1.1 constant_dynamic-update-slice_fusion
  12.4 6.4 %gather_fusion = bf16[128,64,512]{2,1,0:T(8,128)(2,1)} fusion(bf16[17,64,512]{2,1,0:T(8,128)(2,1)S(1)} %bitcast.52, s32[1024]{0:T(1024)S(1)} %pad_clamp_fusion.1), kind=kCustom, calls=%fused_computation | custom fusion | bytes 16777728 | tf_op jit(solution)/shard_map/jit(_take)/gather | solution.py:96
  18.8 7.5 %select_select_fusion = bf16[64,2,64,512]{3,2,1,0:T(8,128)(2,1)} fusion(bf16[64,2,64,512]{3,2,1,0:T(8,128)(2,1)} %bitcast.55, pred[64,2]{1,0:T(8,128)(4,1)S(1)} %copy.60, pred[64,2]{1,0:T(8,128)(4,1)S(1)} %copy.57), kind=kLoop, calls=%fused_computation.2 | loop fusion | flops 8388608 | bytes 16777472 | tf_op jit(solution)/shard_map/jit(_where)/select_n | solution.py:99
  26.3 11.6 %all-to-all-start = ((bf16[64,2,64,512]{3,2,1,0:T(8,128)(2,1)}), bf16[64,2,64,512]{3,2,1,0:T(8,128)(2,1)}, u32[]{:S(2)}, u32[]{:S(2)}) async-start(bf16[64,2,64,512]{3,2,1,0:T(8,128)(2,1)} %select_select_fusion), calls=%async_computation | async-start | bytes 16777216 | tf_op jit(solution)/shard_map/all_to_all | solution.py:100
  38.0 2.1 collective-permute-start
  40.0 5.6 %collective-permute-start.1 = (bf16[64,512]{1,0:T(8,128)(2,1)S(1)}, bf16[64,512]{1,0:T(8,128)(2,1)S(1)}, u32[]{:S(2)}, u32[]{:S(2)}) collective-permute-start(bf16[64,512]{1,0:T(8,128)(2,1)S(1)} %get-tuple-element.15), channel_id=1, source_target_pairs={{8,0},{16,8},{24,16},{32,24},{40,32},{48,40},{56,48},{64,56},{72,6... | collective-permute-start | bytes 196616 | tf_op jit(solution)/shard_map/ppermute | solution.py:23
  45.7 0.6 fusion.21
  49.9 0.7 dynamic-slice_select_fusion.1
  50.8 0.8 broadcast_multiply_fusion
  52.5 2.5 reshape_reshape.3
  55.0 214.2 %all-reduce.3.cloned.1.call-done = (bf16[1,64,512]{2,1,0:T(8,128)(2,1)}, bf16[1,64,512]{2,1,0:T(8,128)(2,1)}) async-done(((bf16[1,64,512]{2,1,0:T(8,128)(2,1)}, bf16[1,64,512]{2,1,0:T(8,128)(2,1)}), (bf16[1,64,512]{2,1,0:T(8,128)(2,1)}, bf16[1,64,512]{2,1,0:T(8,128)(2,1)})) %all-reduce.3.cloned.1.call-update) | async-done | bytes 131088 | tf_op jit(solution)/shard_map/psum | solution.py:30
  269.1 0.9 pad_maximum_fusion.2
  270.2 1.1 constant_dynamic-update-slice_fusion.4
  271.3 1.1 constant_dynamic-update-slice_fusion.3
  272.3 1.1 constant_dynamic-update-slice_fusion.2
  273.4 1.7 broadcast_dynamic-update-slice_fusion
  275.1 5.9 %gather_fusion.1 = bf16[51,64,512]{2,1,0:T(8,128)(2,1)} fusion(bf16[128,64,512]{2,1,0:T(8,128)(2,1)} %bitcast.12, s32[1024]{0:T(1024)S(1)} %pad_clamp_fusion), kind=kCustom, calls=%fused_computation.1 | custom fusion | bytes 6684876 | tf_op jit(solution)/shard_map/jit(_take)/gather | solution.py:110
  281.0 5.2 %select_dynamic-update-slice_fusion = bf16[17,8,64,512]{3,2,1,0:T(8,128)(2,1)} fusion(bf16[17,8,64,512]{3,2,1,0:T(8,128)(2,1)} %broadcast_dynamic-update-slice_fusion, bf16[17,3,64,512]{3,2,1,0:T(8,128)(2,1)} %bitcast.57, pred[17,3]{1,0:T(8,128)(4,1)S(1)} %copy.52), kind=kLoop, calls=%fused_computation.8 | loop fusion | flops 1671168 | bytes 6684723 | tf_op jit(solution)/shard_map/concatenate | solution.py:115
  286.2 8.1 %fusion.19 = (bf16[17,512,256]{2,1,0:T(8,128)(2,1)}, bf16[17,512,256]{2,1,0:T(8,128)(2,1)}) fusion(bf16[17,512,512]{2,1,0:T(8,128)(2,1)} %bitcast.16), kind=kLoop, calls=%fused_computation.51 | loop fusion | bytes 17825792 | tf_op jit(solution)/shard_map/slice | solution.py:40
  294.2 6.5 %copy.64 = bf16[17,512,256]{1,2,0:T(8,128)(2,1)} copy(bf16[17,512,256]{2,1,0:T(8,128)(2,1)} %get-tuple-element.9) | data formatting | bytes 8912896 | tf_op jit(solution)/shard_map/slice | solution.py:40
  300.7 6.6 %copy.63 = bf16[17,512,256]{1,2,0:T(8,128)(2,1)} copy(bf16[17,512,256]{2,1,0:T(8,128)(2,1)} %get-tuple-element.10) | data formatting | bytes 8912896 | tf_op jit(solution)/shard_map/slice | solution.py:53
  307.4 3.4 bitcast_reduce_fusion
  310.8 1.3 fusion.1
  312.1 2.0 divide_convert_fusion
  314.2 0.6 copy.68
  314.8 0.9 copy.78
  315.7 68.1 %all-gather.2.cloned.1.call-done = bf16[1088,2048]{1,0:T(8,128)(2,1)} async-done(((bf16[1088,256]{1,0:T(8,128)(2,1)}), bf16[1088,2048]{1,0:T(8,128)(2,1)}) %all-gather.2.cloned.1.call-update) | async-done | bytes 4456464 | tf_op jit(solution)/shard_map/all_gather | solution.py:120
  383.7 5.7 %convolution_convert_fusion = bf16[1088,512]{1,0:T(8,128)(2,1)} fusion(bf16[1088,2048]{1,0:T(8,128)(2,1)} %all-gather.2.cloned.1.call-done, bf16[2048,512]{1,0:T(8,128)(2,1)S(1)} %copy-done), kind=kOutput, calls=%fused_computation.9 | convolution fusion | flops 2282258432 | bytes 7667712 | tf_op jit(solution)/shard_map/dot_general | solution.py:119
  (48 shorter events, 2.9 us)
Async XLA Ops:
  6.5 377.2 %copy-start = (bf16[2048,512]{1,0:T(8,128)(2,1)S(1)}, bf16[2048,512]{1,0:T(8,128)(2,1)}, u32[]{:S(2)}) copy-start(bf16[2048,512]{1,0:T(8,128)(2,1)} %param.13) | copy-start | bytes 6291460
  26.3 19.4 %copy-start.2 = (s32[2]{0:T(128)S(1)}, s32[2]{0:T(128)}, u32[]{:S(2)}) copy-start(s32[2]{0:T(128)} %param.12) | copy-start | bytes 28
  26.3 248.8 %all-to-all-start = ((bf16[64,2,64,512]{3,2,1,0:T(8,128)(2,1)}), bf16[64,2,64,512]{3,2,1,0:T(8,128)(2,1)}, u32[]{:S(2)}, u32[]{:S(2)}) async-start(bf16[64,2,64,512]{3,2,1,0:T(8,128)(2,1)} %select_select_fusion), calls=%async_computation | async-start | bytes 16777216 | tf_op jit(solution)/shard_map/all_to_all | solution.py:100
  37.9 231.2 %all-reduce.3.cloned.1.call-start = ((), (), s32[]{:S(2)}) async-start(), calls=%async_computation.2 | async-start | bytes 262144 | tf_op jit(solution)/shard_map/psum | solution.py:30
  38.0 232.1 %collective-permute-start = (bf16[64,512]{1,0:T(8,128)(2,1)S(1)}, bf16[64,512]{1,0:T(8,128)(2,1)S(1)}, u32[]{:S(2)}, u32[]{:S(2)}) collective-permute-start(bf16[64,512]{1,0:T(8,128)(2,1)S(1)} %get-tuple-element.16), channel_id=1, source_target_pairs={{0,8},{8,16},{16,24},{24,32},{32,40},{40,48},{48,56},{56,64},{64,7... | collective-permute-start | bytes 196616 | tf_op jit(solution)/shard_map/ppermute | solution.py:22
  40.0 230.0 %collective-permute-start.1 = (bf16[64,512]{1,0:T(8,128)(2,1)S(1)}, bf16[64,512]{1,0:T(8,128)(2,1)S(1)}, u32[]{:S(2)}, u32[]{:S(2)}) collective-permute-start(bf16[64,512]{1,0:T(8,128)(2,1)S(1)} %get-tuple-element.15), channel_id=1, source_target_pairs={{8,0},{16,8},{24,16},{32,24},{40,32},{48,40},{56,48},{64,56},{72,6... | collective-permute-start | bytes 196616 | tf_op jit(solution)/shard_map/ppermute | solution.py:23
  50.6 333.1 %all-gather.2.cloned.1.call-start = ((), (), s32[]{:S(2)}) async-start(), calls=%async_computation.1 | async-start | bytes 5013504 | tf_op jit(solution)/shard_map/all_gather | solution.py:120
  300.7 6.6 %copy-start.1 = (bf16[17,64,2,128]{3,2,1,0:T(2,128)(2,1)S(1)}, bf16[17,64,2,128]{3,2,1,0:T(2,128)(2,1)}, u32[]{:S(2)}) copy-start(bf16[17,64,2,128]{3,2,1,0:T(2,128)(2,1)} %reshape_reshape.3) | copy-start | bytes 1671172
  307.4 4.7 %slice-start = ((s8[4456448]{0:T(1024)(128)(4,1)}), s8[4194304]{0:T(1024)(128)(4,1)S(1)}, s32[]{:S(2)}) async-start(s8[4456448]{0:T(1024)(128)(4,1)} %bitcast.58), calls=%async_computation.3 | async-start | bytes 8388608
  307.4 4.8 %slice-start.1 = ((s8[4456448]{0:T(1024)(128)(4,1)}), s8[262144]{0:T(1024)(128)(4,1)S(1)}, s32[]{:S(2)}) async-start(s8[4456448]{0:T(1024)(128)(4,1)} %bitcast.58), calls=%async_computation.4 | async-start | bytes 524288
Sparse Core Ops, SparseCore 0:
  50.7 218.3 all-reduce.2
  315.8 67.8 all-gather.1
where the time goes:
time: 398 us; the launch traced here: 396 us
  waiting for transfers between devices  282 us (71%)
  local copies, waits for them, and re-layouts  48.1 us (12%)
  starting transfers between devices  19.6 us (5%)
  other arithmetic  17.9 us (4%)
  between operations  17.3 us (4%)
  matrix products  11.1 us (3%)
    psum x1, waiting for transfers between devices, spread(): return lax.psum(block, axis)  214 us
    all_gather x1, waiting for transfers between devices, on_device(): lax.all_gather(context, 'head', axis=1, tiled=True)  68.1 us
    slice x2, local copies, waits for them, and re-layouts, attend_sets(): key_part = pair_rows[..., :columns].reshape(block_count, -1, head_count, DH)  14.6 us
    all_to_all x1, starting transfers between devices, on_device(): lax.all_to_all(outgoing, 'seq', split_axis=0, concat_axis=0, tiled=True)  11.6 us
  transfers between devices with their start and end apart: 5, of which 2 were waited for; matrix products, arithmetic and copies ran while one was open for 3% of the time, Pallas kernels for 0%

commit v1 on v0

v1 whole, which is shorter than its diff:
```python
import math

import jax
import jax.numpy as jnp
from jax import lax
from jax.experimental import pallas as pl
from jax.experimental.pallas import tpu as pltpu
from jax.sharding import PartitionSpec as P

MESH = pl.DeviceIdType.MESH
DH = 128
BLOCK = 64
R = 3
G = 2
NX, NY, NC, NZ = 4, 8, 2, 8
PER = 17
HEADS = 2
COLS = NX * NC
SLOTS = 2 * NY + G
KEYS = 8 * BLOCK
CUT = 9
PIECES = ((0, CUT), (CUT, PER - CUT))
SCALE = 1.0 / math.sqrt(DH)
STEP_KS = ((0,), (1, 2), (3, 4), (5, 6), (7,))
Y_OF_K = (0, -1, 1, -2, 2, -3, 3, 4)
K_OF_DY = (0, 2, 4, 6, 7, 5, 3, 1)
TILE = 272


def place():
    seq = lax.axis_index("seq")
    return seq // (NY * NC), (seq // NC) % NY, seq % NC, lax.axis_index("head")


def exchange_tables(rand_group, rand_offset, glob_blocks):
    x, y, c, _ = place()
    seq = lax.axis_index("seq")
    count = PER * R
    code = (rand_group * 32 + rand_offset).reshape(NX, NY, NC * count)
    row = lax.dynamic_index_in_dim(code, y, 1, keepdims=False).reshape(COLS, count)
    j = jnp.arange(COLS, dtype=jnp.int32)
    receiver = ((x - j // NC) % NX) * NC + (c - j % NC) % NC
    row = jnp.take(row, receiver, axis=0)
    ys = (y + jnp.array(Y_OF_K, jnp.int32)) % NY
    groups = (x * NY + ys) * NC + c
    match = (row // 32)[:, None, :] == groups[None, :, None]
    ranked = jnp.arange(count, dtype=jnp.int32)[None, :] * 32 + row % 32
    ranked = ranked[:, None, :]
    first = jnp.min(jnp.where(match, ranked, 1 << 12), axis=2) % 32
    last = jnp.max(jnp.where(match, ranked, 0), axis=2) % 32
    send = jnp.stack([first, last], axis=2).reshape(-1)

    k_of_dy = jnp.array(K_OF_DY, jnp.int32)

    def column(group):
        return ((group // (NY * NC) - x) % NX) * NC + (group % NC - c) % NC

    def ring(group):
        dy = ((group // NC) % NY - y) % NY
        return jnp.sum(jnp.where(dy[..., None] == jnp.arange(NY), k_of_dy, 0), axis=-1)

    mine = lax.dynamic_slice_in_dim(rand_group, seq * PER, PER, 0).reshape(-1)
    n = jnp.arange(count, dtype=jnp.int32)
    earlier = (mine[:, None] == mine[None, :]) & (n[None, :] < n[:, None])
    rank = jnp.sum(earlier.astype(jnp.int32), axis=1)
    rand_slots = (column(mine) * SLOTS + 2 * ring(mine) + rank).reshape(PER, R)
    glob_group = glob_blocks // PER
    glob_slots = column(glob_group) * SLOTS + 2 * NY + jnp.arange(G, dtype=jnp.int32)
    read = jnp.concatenate([jnp.broadcast_to(glob_slots[None], (PER, G)), rand_slots], axis=1).reshape(-1)
    cand = jnp.stack([ring(glob_group), glob_blocks % PER], axis=1).reshape(-1)
    return send.astype(jnp.int32), read.astype(jnp.int32), cand.astype(jnp.int32)


def kernel(*refs):
    send_t, read_t, cand_t, q_ref, k_ref, v_ref, w_ref, out_ref, *refs = refs
    y_bufs = [refs[7 * sl : 7 * sl + 7] for sl in range(4)]
    refs = refs[28:]
    stage, land, pads = refs[0:4], refs[4:8], refs[8:12]
    p_bufs, t_bufs, ctx, w_bufs = refs[12:14], refs[14:16], refs[16:18], refs[18:20]
    acc, y_s, y_r, x_s, x_r, h_s, h_r, z_s, z_r, w_s = refs[20:]
    x, y, c, z = place()

    def dev(dx=0, dy=0, dc=0, dz=0):
        return (((x + dx) % NX * NY + (y + dy) % NY) * NC + (c + dc) % NC, (z + dz) % NZ)

    seq = lax.axis_index("seq")
    n_seq = NX * NY * NC
    ahead, behind = ((seq + 1) % n_seq, z), ((seq + n_seq - 1) % n_seq, z)
    y_up, y_down, z_up, z_down = dev(dy=1), dev(dy=NY - 1), dev(dz=1), dev(dz=NZ - 1)
    row = [None] + [dev(dx=NX - j // NC, dc=NC - j % NC) for j in range(1, COLS)]
    order = (4, 5, 2, 3, 6, 7, 1)

    def remote(src, dst, s, r, to):
        return pltpu.make_async_remote_copy(
            src_ref=src, dst_ref=dst, send_sem=s, recv_sem=r, device_id=to, device_id_type=MESH
        )

    peers = [y_up, y_down, z_up, z_down, ahead, behind] + row[1:]
    barrier = pltpu.get_barrier_semaphore()
    for peer in peers:
        pl.semaphore_signal(barrier, inc=1, device_id=peer, device_id_type=MESH)

    w_copies = []
    for h in range(HEADS):
        for k in range(NZ):
            rows = ((z + Y_OF_K[k] + NZ) % NZ * HEADS + h) * DH
            copy = pltpu.make_async_copy(
                w_ref.at[pl.ds(pl.multiple_of(rows, DH), DH)], w_bufs[h].at[pl.ds(k * DH, DH)], w_s.at[h * NZ + k]
            )
            copy.start()
            w_copies.append(copy)

    pl.semaphore_wait(barrier, len(peers))

    def own(sl):
        ref = k_ref if sl < 2 else v_ref
        cols = pl.ds(sl % 2 * DH, DH)
        return ref, cols

    pending = []

    def y_copy(sl, step, up, piece):
        start, size = PIECES[piece]
        blocks = pl.ds(start, size)
        if step == 1:
            ref, cols = own(sl)
            src = ref.at[blocks, :, cols]
        else:
            src = y_bufs[sl][2 * step - (4 if up else 3)].at[blocks]
        dst = y_bufs[sl][6 if step == 4 else 2 * step - (2 if up else 1)].at[blocks]
        n = (step - 1) * 4 + (0 if up else 2) + piece
        return remote(src, dst, y_s.at[sl, n], y_r.at[sl, n], y_up if up else y_down)

    def y_send(sl, step, up, piece):
        if step == 4 and up != (piece == 0):
            return
        copy = y_copy(sl, step, up, piece)
        copy.start()
        pending.append(copy)

    def y_begin(sl):
        for piece in (0, 1):
            for up in (True, False):
                y_send(sl, 1, up, piece)

    def y_step(sl, step):
        for piece in (0, 1):
            for up in (True, False):
                if step == 4 and up != (piece == 0):
                    continue
                y_copy(sl, step, up, piece).wait_recv()
                if step < 4:
                    y_send(sl, step + 1, up, piece)

    def load(sl, k, off):
        if k == 0:
            ref, cols = own(sl)
            return ref[off, :, cols]
        return y_bufs[sl][k - 1][off]

    def x_step(sl, step):
        ks = STEP_KS[step]

        def fill(j, _):
            for k in ks:
                for slot in range(2):
                    off = send_t[j * 2 * NY + 2 * k + slot]
                    stage[sl][(j - 1) * SLOTS + 2 * k + slot] = load(sl, k, off)
            return 0

        lax.fori_loop(1, COLS, fill, 0)
        first, size = 2 * ks[0], 2 * len(ks)
        if step == 4:
            size += G
            for g in range(G):
                at = cand_t[2 * g]
                off = cand_t[2 * g + 1]
                block = load(sl, 0, off)
                for k in range(1, NY):
                    block = jnp.where(at == k, load(sl, k, off), block)
                land[sl][2 * NY + g] = block
                for j in range(1, COLS):
                    stage[sl][(j - 1) * SLOTS + 2 * NY + g] = block
        for j in order:
            remote(
                stage[sl].at[pl.ds((j - 1) * SLOTS + first, size)],
                land[sl].at[pl.ds(j * SLOTS + first, size)],
                x_s.at[sl],
                x_r.at[sl],
                row[j],
            ).start()
        for k in ks:
            for slot in range(2):
                land[sl][2 * k + slot] = load(sl, k, send_t[2 * k + slot])

    def x_whole(sl):
        return remote(
            stage[sl].at[...], land[sl].at[pl.ds(SLOTS, (COLS - 1) * SLOTS)], x_s.at[sl], x_r.at[sl], row[1]
        )

    halo = []

    def edges(sl):
        ref, cols = own(sl)
        for n, (src, dst, to) in enumerate(((PER - 1, 0, ahead), (0, PER + 1, behind))):
            copy = remote(ref.at[src, :, cols], pads[sl].at[dst], h_s.at[sl, n], h_r.at[sl, n], to)
            copy.start()
            halo.append(copy)

        def fill(i, _):
            pads[sl][i + 1] = ref[i, :, cols]
            return 0

        lax.fori_loop(0, PER, fill, 0)

    def edges_wait(sl):
        for n in range(2):
            halo[2 * sl + n].wait_recv()

    def gathered(sl, i):
        return jnp.concatenate(
            [pads[sl][i], pads[sl][i + 1], pads[sl][i + 2]]
            + [land[sl][read_t[(G + R) * i + n]] for n in range(G + R)],
            axis=0,
        )

    def scores(h, start, stop):
        def one(i, _):
            s = lax.dot_general(
                q_ref[i, :, pl.ds(h * DH, DH)],
                gathered(h, i),
                (((1,), (1,)), ((), ())),
                preferred_element_type=jnp.float32,
            )
            s = s * SCALE
            e = jnp.exp(s - jnp.max(s, axis=1, keepdims=True))
            t_bufs[h][i] = jnp.broadcast_to(jnp.sum(e, axis=1, keepdims=True), (BLOCK, DH))
            p_bufs[h][i] = e.astype(jnp.bfloat16)
            return 0

        lax.fori_loop(start, stop, one, 0)

    def context(h, start, stop):
        def one(i, _):
            o = jnp.dot(p_bufs[h][i], gathered(2 + h, i), preferred_element_type=jnp.float32)
            rows = pl.ds(pl.multiple_of(i * BLOCK, BLOCK), BLOCK)
            ctx[h][rows, pl.ds(0, DH)] = (o / t_bufs[h][i]).astype(jnp.bfloat16)
            return 0

        lax.fori_loop(start, stop, one, 0)

    ROWS = PER * BLOCK
    Z_PIECES = ((0, CUT * BLOCK), (CUT * BLOCK, ROWS - CUT * BLOCK))

    def z_copy(h, step, up, piece):
        rows = pl.ds(*Z_PIECES[piece])
        from_k = 0 if step == 1 else 2 * step - (3 if up else 2)
        to_k = 7 if step == 4 else 2 * step - (1 if up else 0)
        n = (step - 1) * 4 + (0 if up else 2) + piece
        return remote(
            ctx[h].at[rows, pl.ds(from_k * DH, DH)],
            ctx[h].at[rows, pl.ds(to_k * DH, DH)],
            z_s.at[h, n],
            z_r.at[h, n],
            z_up if up else z_down,
        )

    def z_send(h, step, up, piece):
        if step == 4 and up != (piece == 0):
            return
        copy = z_copy(h, step, up, piece)
        copy.start()
        pending.append(copy)

    def z_begin(h, piece):
        for up in (True, False):
            z_send(h, 1, up, piece)

    def z_step(h, step):
        for piece in (0, 1):
            for up in (True, False):
                if step == 4 and up != (piece == 0):
                    continue
                z_copy(h, step, up, piece).wait_recv()
                if step < 4:
                    z_send(h, step + 1, up, piece)

    def project(h, k0, k1, first=False, last=False):
        cols = pl.ds(k0 * DH, (k1 - k0) * DH)

        def tile(n, _):
            rows = pl.ds(pl.multiple_of(n * TILE, 16), TILE)
            part = jnp.dot(ctx[h][rows, cols], w_bufs[h][cols, :], preferred_element_type=jnp.float32)
            if not first:
                part = part + acc[rows, :]
            if last:
                out_ref[rows, :] = part.astype(out_ref.dtype)
            else:
                acc[rows, :] = part
            return 0

        lax.fori_loop(0, ROWS // TILE, tile, 0)

    y_begin(0)
    for sl in range(2):
        edges(sl)
    x_step(0, 0)

    y_step(0, 1)
    x_step(0, 1)
    edges(2)
    y_step(0, 2)
    x_step(0, 2)
    edges(3)
    y_step(0, 3)
    y_begin(1)
    x_step(0, 3)
    y_step(0, 4)
    x_step(0, 4)
    x_step(1, 0)

    y_step(1, 1)
    x_step(1, 1)
    y_step(1, 2)
    x_step(1, 2)
    edges_wait(0)
    x_whole(0).wait_recv()
    scores(0, 0, 4)
    y_step(1, 3)
    y_begin(2)
    x_step(1, 3)
    scores(0, 4, 9)
    y_step(1, 4)
    x_step(1, 4)
    x_step(2, 0)
    scores(0, 9, 13)

    y_step(2, 1)
    x_step(2, 1)
    scores(0, 13, 17)
    y_step(2, 2)
    x_step(2, 2)
    edges_wait(1)
    x_whole(1).wait_recv()
    scores(1, 0, 4)
    y_step(2, 3)
    y_begin(3)
    x_step(2, 3)
    scores(1, 4, 9)
    y_step(2, 4)
    x_step(2, 4)
    x_step(3, 0)
    scores(1, 9, 13)

    y_step(3, 1)
    x_step(3, 1)
    scores(1, 13, 17)
    edges_wait(2)
    edges_wait(3)
    y_step(3, 2)
    x_step(3, 2)
    x_whole(2).wait_recv()
    context(0, 0, CUT)
    z_begin(0, 0)
    context(0, CUT, PER)
    z_begin(0, 1)
    y_step(3, 3)
    x_step(3, 3)
    z_step(0, 1)
    y_step(3, 4)
    x_step(3, 4)
    z_step(0, 2)
    x_whole(3).wait_recv()
    context(1, 0, CUT)
    z_begin(1, 0)
    context(1, CUT, PER)
    z_begin(1, 1)
    z_step(0, 3)
    for copy in w_copies:
        copy.wait()
    z_step(0, 4)
    z_step(1, 1)
    project(0, 0, 8, first=True)
    z_step(1, 2)
    project(1, 0, 4)
    z_step(1, 3)
    project(1, 4, 6)
    z_step(1, 4)
    project(1, 6, 8, last=True)

    for copy in pending:
        copy.wait_send()
    for copy in halo:
        copy.wait_send()
    for sl in range(4):
        x_whole(sl).wait_send()


def on_device(queries, keys, values, rand_group, rand_offset, glob_blocks, w_out):
    tables = exchange_tables(rand_group, rand_offset, glob_blocks)
    shape = (PER, BLOCK, HEADS * DH)
    bf16 = jnp.bfloat16
    group = pltpu.VMEM((PER, BLOCK, DH), bf16)
    scratch = [group] * 28
    scratch += [pltpu.VMEM(((COLS - 1) * SLOTS, BLOCK, DH), bf16)] * 4
    scratch += [pltpu.VMEM((COLS * SLOTS, BLOCK, DH), bf16)] * 4
    scratch += [pltpu.VMEM((PER + 2, BLOCK, DH), bf16)] * 4
    scratch += [pltpu.VMEM((PER, BLOCK, KEYS), bf16)] * 2
    scratch += [pltpu.VMEM((PER, BLOCK, DH), jnp.float32)] * 2
    scratch += [pltpu.VMEM((PER * BLOCK, NZ * DH), bf16)] * 2
    scratch += [pltpu.VMEM((NZ * DH, w_out.shape[1]), bf16)] * 2
    scratch += [pltpu.VMEM((PER * BLOCK, w_out.shape[1]), jnp.float32)]
    dma = pltpu.SemaphoreType.DMA
    scratch += [dma((4, 16)), dma((4, 16)), dma((4,)), dma((4,)), dma((4, 2)), dma((4, 2))]
    scratch += [dma((2, 16)), dma((2, 16)), dma((2 * NZ,))]
    smem = pl.BlockSpec(memory_space=pltpu.SMEM)
    vmem = pl.BlockSpec(memory_space=pltpu.VMEM)
    return pl.pallas_call(
        kernel,
        out_shape=jax.ShapeDtypeStruct((PER * BLOCK, w_out.shape[1]), bf16),
        in_specs=[smem, smem, smem, vmem, vmem, vmem, pl.BlockSpec(memory_space=pl.ANY)],
        out_specs=vmem,
        scratch_shapes=scratch,
        compiler_params=pltpu.CompilerParams(collective_id=0, has_side_effects=True, vmem_limit_bytes=60 << 20),
        name="sparse_attention",
    )(*tables, queries.reshape(shape), keys.reshape(shape), values.reshape(shape), w_out)


def solution(mesh):
    return jax.shard_map(
        on_device,
        mesh=mesh,
        in_specs=(P("seq", "head"), P("seq", "head"), P("seq", "head"), P(), P(), P(), P(None, "head")),
        out_specs=P("seq", "head"),
        check_vma=False,
    )
```

time: 398 us -> 171 us (0.43)
  waiting for transfers between devices: 282 us -> 0 us
  Pallas kernels: 0 us -> 160 us
  local copies, waits for them, and re-layouts: 48.1 us -> 6.64 us
  starting transfers between devices: 19.6 us -> 0 us
  between operations: 17.3 us -> 0.09 us
  other arithmetic: 17.9 us -> 4.61 us
  matrix products: 11.1 us -> 0 us
    psum x1 -> x0, waiting for transfers between devices: 214 us -> none  [spread(): return lax.psum(block, axis)]
    pallas_call x0 -> x1, Pallas kernels: none -> 160 us  [on_device(): pl.pallas_call(kernel, out_shape=jax.ShapeDtypeStruct((PER * BLOCK, w_out...]
    all_gather x1 -> x0, waiting for transfers between devices: 68.1 us -> none  [on_device(): lax.all_gather(context, 'head', axis=1, tiled=True)]
    slice x5 -> x0, local copies, waits for them, and re-layouts: 21.8 us -> none  [the longest x2 14.6 us: attend_sets(): key_part = pair_rows[..., :columns].reshape(block_count, -1, head_count, DH)]
    gather x2 -> x1, local copies, waits for them, and re-layouts: 12.3 us -> 0.55 us  [exchange_tables(): row = jnp.take(row, receiver, axis=0)]
    all_to_all x1 -> x0, starting transfers between devices: 11.6 us -> none  [on_device(): lax.all_to_all(outgoing, 'seq', split_axis=0, concat_axis=0, tiled=True)]
    dot_general x3 -> x0, matrix products: 11.1 us -> none  [the longest x1 5.73 us: on_device(): jnp.dot(lax.all_gather(context, 'head', axis=1, tiled=True), w_out, prefe...]
    ppermute x2 -> x0, starting transfers between devices: 7.67 us -> none  [the longest x1 5.61 us: padded_2(): after = lax.ppermute(initial, axis, down)]
  transfers between devices with their start and end apart: 5 -> 0, of which waited for: 2 -> 0; matrix products, arithmetic and copies ran while one was open for 3% -> 0% of each run, Pallas kernels for 0% -> 0%
where the time goes in v1:
time: 171 us
  Pallas kernels  160 us (94%)
  local copies, waits for them, and re-layouts  6.64 us (4%)
  other arithmetic  4.61 us (3%)
    pallas_call x1, Pallas kernels, on_device(): pl.pallas_call(kernel, out_shape=jax.ShapeDtypeStruct((PER * BLOCK, w_out...  160 us

profile of v1, /device:TPU:6, one launch (start us, length us, event | category | flops | bytes accessed | tf_op | source)
XLA Modules:
  0.0 170.9 jit_solution(12335034587255750187)
XLA Ops:
  0.0 0.7 fusion.28
  0.7 0.8 constant_dynamic-slice_fusion
  1.5 0.7 and_select_fusion.1
  2.2 0.8 fusion.19
  3.0 0.1 copy.26
  3.1 0.7 reshape.375.refs_2_
  3.8 0.1 copy.27
  3.9 0.1 reshape.373
  4.1 0.2 convert_reduce_fusion
  4.2 0.7 select_reduce_fusion
  5.0 0.1 mul.79
  5.1 0.1 reduce_sum.31
  5.1 0.1 fusion.10
  5.2 0.1 pad_add_fusion
  5.3 0.6 reshape.374.refs_1_
  5.9 0.7 multiply_add_fusion
  6.6 0.2 copy.23
  6.8 0.2 reshape.370
  7.1 0.1 reshape.371
  7.2 0.6 gather_fusion
  7.7 0.1 add_select_fusion.7
  7.8 0.4 fusion
  8.3 0.1 copy.24
  8.4 0.7 reshape.372.refs_0_
  9.0 159.6 %sparse_attention.1 = bf16[1088,512]{1,0:T(8,128)(2,1)} custom-call(s32[128]{0:T(128)} %reshape.372.refs_0_, s32[85]{0:T(128)} %reshape.374.refs_1_, s32[4]{0:T(128)} %reshape.375.refs_2_, bf16[17,64,256]{2,1,0:T(8,128)(2,1)} %bitcast.16, bf16[17,64,256]{2,1,0:T(8,128)(2,1)} %bitcast.17, bf16[17,64,256]{2,1,0:T(8,128)(2,1)} %bitcast.18, ...), custom_call_target="tpu_custom_call" | custom-call | tf_op jit(solution)/shard_map/sparse_attention/pallas_call | solution.py:418
  168.6 2.3 %copy.29 = bf16[1088,512]{1,0:T(8,128)(2,1)} copy(bf16[1088,512]{1,0:T(8,128)(2,1)} %sparse_attention.1) | data formatting | bytes 2228224
  (12 shorter events, 0.2 us)

commit v2 on v0

v2 whole, which is shorter than its diff:
```python
import math

import jax
import jax.numpy as jnp
from jax import lax
from jax.experimental import pallas as pl
from jax.experimental.pallas import tpu as pltpu
from jax.sharding import PartitionSpec as P

MESH = pl.DeviceIdType.MESH
DH = 128
BLOCK = 64
HALF = 32
R = 3
G = 2
NX, NY, NC, NZ = 4, 8, 2, 8
PER = 17
ROWS = PER * BLOCK
HEADS = 2
COLS = NX * NC
SLOTS = 2 * NY
KEYS = 8 * BLOCK
CUT = 9
PIECES = ((0, CUT), (CUT, PER - CUT))
SCALE = 1.0 / math.sqrt(DH)
STEP_KS = ((0,), (1, 2), (3, 4), (5, 6), (7,))
Y_OF_K = (0, -1, 1, -2, 2, -3, 3, 4)
K0, V0, K1, V1A, V1B = range(5)
HEIGHT = (BLOCK, BLOCK, BLOCK, HALF, HALF)
TILE = 272
BF16 = jnp.bfloat16


def place():
    seq = lax.axis_index("seq")
    return seq // (NY * NC), (seq // NC) % NY, seq % NC, lax.axis_index("head")


def kernel(*refs):
    glob, code_ref, q_hbm, k_hbm, v_hbm, w_ref, out_ref, *refs = refs
    q_ref, k_ref, v_ref, send_v, read_v, send_t, read_t, *refs = refs
    y_bufs = [refs[7 * sl : 7 * sl + 7] for sl in range(5)]
    refs = refs[35:]
    stage, land, pads, g_out, g_in, g_sel, g_other, g_fin = [refs[5 * n : 5 * n + 5] for n in range(8)]
    refs = refs[40:]
    packed, p_bufs, t_bufs, ctx, w_hi, refs = refs[0:2], refs[2:4], refs[4:6], refs[6:9], refs[9:11], refs[11:]
    w_lo, refs = refs[0:3], refs[3:]
    acc, y_s, y_r, x_s, x_r, g_s, g_r, c_s, c_r, h_s, h_r, z_s, z_r, w_s, i_s = refs
    x, y, c, z = place()
    seq = lax.axis_index("seq")

    def dev(dx=0, dy=0, dc=0, dz=0):
        return (((x + dx) % NX * NY + (y + dy) % NY) * NC + (c + dc) % NC, (z + dz) % NZ)

    n_seq = NX * NY * NC
    ahead, behind = ((seq + 1) % n_seq, z), ((seq + n_seq - 1) % n_seq, z)
    y_up, y_down, z_up, z_down = dev(dy=1), dev(dy=NY - 1), dev(dz=1), dev(dz=NZ - 1)
    row = [dev(dx=NX - j // NC, dc=NC - j % NC) for j in range(COLS)]
    order = (4, 5, 2, 3, 6, 7, 1)

    def remote(src, dst, s, r, to):
        return pltpu.make_async_remote_copy(
            src_ref=src, dst_ref=dst, send_sem=s, recv_sem=r, device_id=to, device_id_type=MESH
        )

    peers = [y_up, y_down, z_up, z_down, ahead, behind] + row[1:]
    barrier = pltpu.get_barrier_semaphore()
    for peer in peers:
        pl.semaphore_signal(barrier, inc=1, device_id=peer, device_id_type=MESH)

    in_copies = [
        pltpu.make_async_copy(src, dst, i_s.at[n])
        for n, (src, dst) in enumerate(((k_hbm, k_ref), (v_hbm, v_ref), (q_hbm, q_ref)))
    ]
    for copy in in_copies:
        copy.start()

    w_copies = []

    def w_copy(start, size, dst):
        copy = pltpu.make_async_copy(w_ref.at[pl.ds(pl.multiple_of(start, HALF), size)], dst, w_s.at[len(w_copies)])
        copy.start()
        w_copies.append(copy)

    def w_begin():
        for k in range(NZ):
            at = (z + Y_OF_K[k] + NZ) % NZ * (HEADS * DH)
            w_copy(at, DH, w_lo[0].at[pl.ds(k * DH, DH)])
            for a in range(2):
                w_copy(at + DH + a * BLOCK, BLOCK, w_lo[1 + a].at[pl.ds(k * DH, BLOCK)])
                w_copy(at + DH + a * BLOCK, BLOCK, w_hi[a].at[pl.ds(k * DH + BLOCK, BLOCK)])

    def w_zeros():
        zeros = jnp.zeros((BLOCK, w_ref.shape[1]), BF16)
        for a in range(2):
            for k in range(NZ):
                w_lo[1 + a][pl.ds(k * DH + BLOCK, BLOCK), :] = zeros
                w_hi[a][pl.ds(k * DH, BLOCK), :] = zeros

    in_copies[0].wait()
    pl.semaphore_wait(barrier, len(peers))

    def source(sl, blocks):
        if sl in (K0, K1):
            return k_ref.at[blocks, :, pl.ds(DH if sl == K1 else 0, DH)]
        if sl == V0:
            return v_ref.at[blocks, :, pl.ds(0, DH)]
        return packed[sl - V1A].at[blocks]

    def load(sl, k, off):
        if k:
            return y_bufs[sl][k - 1][off]
        if sl in (K0, K1):
            return k_ref[off, :, pl.ds(DH if sl == K1 else 0, DH)]
        if sl == V0:
            return v_ref[off, :, pl.ds(0, DH)]
        return packed[sl - V1A][off]

    pending = []

    def start(copy):
        copy.start()
        pending.append(copy)

    def y_copy(sl, step, up, piece):
        blocks = pl.ds(*PIECES[piece])
        if step == 1:
            src = source(sl, blocks)
        else:
            src = y_bufs[sl][2 * step - (4 if up else 3)].at[blocks]
        dst = y_bufs[sl][6 if step == 4 else 2 * step - (2 if up else 1)].at[blocks]
        n = (step - 1) * 4 + (0 if up else 2) + piece
        return remote(src, dst, y_s.at[sl, n], y_r.at[sl, n], y_up if up else y_down)

    def moves(step):
        return [(piece, up) for piece in (0, 1) for up in (True, False) if step < 4 or (step == 4 and up == (piece == 0))]

    def y_begin(sl):
        for piece, up in moves(1):
            start(y_copy(sl, 1, up, piece))

    def y_step(sl, step):
        for piece, up in moves(step):
            y_copy(sl, step, up, piece).wait_recv()
            if (piece, up) in moves(step + 1):
                start(y_copy(sl, step + 1, up, piece))

    def x_step(sl, step):
        ks = STEP_KS[step]
        first, size = 2 * ks[0], 2 * len(ks)

        def fill(j, _):
            for k in ks:
                for slot in range(2):
                    stage[sl][(j - 1) * SLOTS + 2 * k + slot] = load(sl, k, send_t[j, 2 * k + slot])
            return 0

        lax.fori_loop(1, COLS, fill, 0)
        for j in order:
            remote(
                stage[sl].at[pl.ds((j - 1) * SLOTS + first, size)],
                land[sl].at[pl.ds(j * SLOTS + first, size)],
                x_s.at[sl],
                x_r.at[sl],
                row[j],
            ).start()
        for k in ks:
            for slot in range(2):
                land[sl][2 * k + slot] = load(sl, k, send_t[0, 2 * k + slot])

    def x_whole(sl):
        return remote(
            stage[sl].at[...], land[sl].at[pl.ds(SLOTS, (COLS - 1) * SLOTS)], x_s.at[sl], x_r.at[sl], row[1]
        )

    glob_at = []
    for g in range(G):
        block = glob[g]
        group = block // PER
        dy_g = (group // NC) % NY + NY - y
        dy_g = jnp.where(dy_g >= NY, dy_g - NY, dy_g)
        k_g = jnp.where(dy_g < 4, 2 * dy_g, jnp.where(dy_g == 4, 7, 15 - 2 * dy_g))
        dx_g = group // (NY * NC) + NX - x
        dx_g = jnp.where(dx_g >= NX, dx_g - NX, dx_g)
        glob_at.append((k_g, block % PER, dx_g, group % NC))

    def g_begin(sl):
        for g, (k_g, off, _, _) in enumerate(glob_at):
            block = load(sl, 0, off)
            for k in range(1, NY):
                block = jnp.where(k_g == k, load(sl, k, off), block)
            g_out[sl][g] = block
        for dx in (2, 1, 3):
            remote(g_out[sl], g_in[sl].at[pl.ds((dx - 1) * G, G)], g_s.at[sl], g_r.at[sl], row[dx * NC]).start()

    def g_whole(sl):
        return remote(g_in[sl], g_in[sl], g_s.at[sl], g_r.at[sl], row[NC])

    def g_cores(sl):
        return remote(g_sel[sl], g_other[sl], c_s.at[sl], c_r.at[sl], row[1])

    def g_mid(sl):
        g_whole(sl).wait_recv()
        for g, (_, _, dx_g, _) in enumerate(glob_at):
            block = g_out[sl][g]
            for dx in (1, 2, 3):
                block = jnp.where(dx_g == dx, g_in[sl][(dx - 1) * G + g], block)
            g_sel[sl][g] = block
        g_cores(sl).start()

    def g_end(sl):
        g_cores(sl).wait_recv()
        for g, (_, _, _, c_g) in enumerate(glob_at):
            g_fin[sl][g] = jnp.where(c_g == c, g_sel[sl][g], g_other[sl][g])

    halo = [[] for _ in range(5)]

    def edges(sl):
        for n, (src, dst, to) in enumerate(((PER - 1, 0, ahead), (0, PER + 1, behind))):
            copy = remote(source(sl, src), pads[sl].at[dst], h_s.at[sl, n], h_r.at[sl, n], to)
            copy.start()
            halo[sl].append(copy)

        def fill(i, _):
            pads[sl][i + 1] = load(sl, 0, i)
            return 0

        lax.fori_loop(0, PER, fill, 0)

    def ready(sl):
        for copy in halo[sl]:
            copy.wait_recv()
        x_whole(sl).wait_recv()
        g_end(sl)

    def pack():
        low = lax.broadcasted_iota(jnp.int32, (HALF, DH), 1) < BLOCK

        def one(i, _):
            top = v_ref[i, pl.ds(0, HALF), pl.ds(DH, DH)].astype(jnp.float32)
            bottom = v_ref[i, pl.ds(HALF, HALF), pl.ds(DH, DH)].astype(jnp.float32)
            packed[0][i] = jnp.where(low, top, pltpu.roll(bottom, BLOCK, 1)).astype(BF16)
            packed[1][i] = jnp.where(low, pltpu.roll(top, BLOCK, 1), bottom).astype(BF16)
            return 0

        lax.fori_loop(0, PER, one, 0)

    def gathered(sl, i):
        return (
            [pads[sl][i], pads[sl][i + 1], pads[sl][i + 2]]
            + [g_fin[sl][g] for g in range(G)]
            + [land[sl][read_t[0, n * 32 + i]] for n in range(R)]
        )

    def scores(h, begin, end):
        def one(i, _):
            blocks = gathered(K1 if h else K0, i)
            if h:
                blocks = [b[:HALF] for b in blocks] + [b[HALF:] for b in blocks]
            s = lax.dot_general(
                q_ref[i, :, pl.ds(h * DH, DH)],
                jnp.concatenate(blocks, axis=0),
                (((1,), (1,)), ((), ())),
                preferred_element_type=jnp.float32,
            )
            s = s * SCALE
            e = jnp.exp(s - jnp.max(s, axis=1, keepdims=True))
            t_bufs[h][i] = jnp.broadcast_to(jnp.sum(e, axis=1, keepdims=True), (BLOCK, DH))
            p_bufs[h][i] = e.astype(BF16)
            return 0

        lax.fori_loop(begin, end, one, 0)

    def context0(begin, end):
        def one(i, _):
            o = jnp.dot(p_bufs[0][i], jnp.concatenate(gathered(V0, i), axis=0), preferred_element_type=jnp.float32)
            rows = pl.ds(pl.multiple_of(i * BLOCK, BLOCK), BLOCK)
            ctx[0][rows, pl.ds(0, DH)] = (o / t_bufs[0][i]).astype(BF16)
            return 0

        lax.fori_loop(begin, end, one, 0)

    def context1(a, begin, end):
        low = lax.broadcasted_iota(jnp.int32, (HALF, DH), 1) < BLOCK
        half_keys = KEYS // 2

        def one(i, _):
            p = jnp.concatenate([p_bufs[1][i, :, pl.ds(0, half_keys)], p_bufs[1][i, :, pl.ds(half_keys, half_keys)]])
            o = jnp.dot(p, jnp.concatenate(gathered(V1A + a, i), axis=0), preferred_element_type=jnp.float32)
            upper = o[0:HALF] + pltpu.roll(o[BLOCK : BLOCK + HALF], BLOCK, 1)
            lower = pltpu.roll(o[HALF:BLOCK], BLOCK, 1) + o[BLOCK + HALF :]
            total = jnp.where(low, t_bufs[1][i, pl.ds(0, HALF)], t_bufs[1][i, pl.ds(HALF, HALF)])
            rows = pl.ds(pl.multiple_of(i * HALF, HALF), HALF)
            ctx[1 + a][rows, pl.ds(0, DH)] = (jnp.where(low, upper, lower) / total).astype(BF16)
            return 0

        lax.fori_loop(begin, end, one, 0)

    def z_copy(t, step, up, piece):
        height = HALF if t else BLOCK
        first, size = PIECES[piece]
        rows = pl.ds(first * height, size * height)
        from_k = 0 if step == 1 else 2 * step - (3 if up else 2)
        to_k = 7 if step == 4 else 2 * step - (1 if up else 0)
        n = (step - 1) * 4 + (0 if up else 2) + piece
        return remote(
            ctx[t].at[rows, pl.ds(from_k * DH, DH)],
            ctx[t].at[rows, pl.ds(to_k * DH, DH)],
            z_s.at[t, n],
            z_r.at[t, n],
            z_up if up else z_down,
        )

    def z_begin(t, piece):
        for up in (True, False):
            start(z_copy(t, 1, up, piece))

    def z_step(t, step, only=None):
        for piece, up in moves(step):
            if only is not None and piece != only:
                continue
            z_copy(t, step, up, piece).wait_recv()
            if (piece, up) in moves(step + 1):
                start(z_copy(t, step + 1, up, piece))

    def project0():
        def tile(n, _):
            rows = pl.ds(pl.multiple_of(n * TILE, 16), TILE)
            acc[rows, :] = jnp.dot(ctx[0][rows, :], w_lo[0][...], preferred_element_type=jnp.float32)
            return 0

        lax.fori_loop(0, ROWS // TILE, tile, 0)

    def project1(a, k0, k1, last=False):
        cols = pl.ds(k0 * DH, (k1 - k0) * DH)
        for b0, b1 in ((0, 6), (6, 12), (12, PER)):
            lhs = ctx[1 + a][pl.ds(b0 * HALF, (b1 - b0) * HALF), cols]
            for w, shift in ((w_lo[1 + a], 0), (w_hi[a], HALF)):
                part = jnp.dot(lhs, w[cols, :], preferred_element_type=jnp.float32)
                for b in range(b0, b1):
                    rows = pl.ds(b * BLOCK + shift, HALF)
                    total = acc[rows, :] + part[(b - b0) * HALF : (b - b0 + 1) * HALF]
                    if last:
                        out_ref[rows, :] = total.astype(out_ref.dtype)
                    else:
                        acc[rows, :] = total

    def tables():
        lane = lax.broadcasted_iota(jnp.int32, (COLS, DH), 1)

        def requests(holders):
            rs = [jnp.concatenate([code_ref[r, pl.ds(at, 1), :] for at in holders], axis=0) for r in range(R)]
            return jnp.where(lane < 32, rs[0], jnp.where(lane < 64, pltpu.roll(rs[1], 32, 1), pltpu.roll(rs[2], 64, 1)))

        asked = requests([row[j][0] for j in range(COLS)])
        ranked = lane * 32 + (asked & 31)
        asked = asked >> 5
        table = jnp.zeros((COLS, DH), jnp.int32)
        for k in range(NY):
            match = asked == dev(dy=Y_OF_K[k] + NY)[0]
            first = jnp.min(jnp.where(match, ranked, 1 << 12), axis=1, keepdims=True) & 31
            last = jnp.max(jnp.where(match, ranked, 0), axis=1, keepdims=True) & 31
            table = jnp.where(lane == 2 * k, first, jnp.where(lane == 2 * k + 1, last, table))
        send_v[...] = table
        mine = requests([seq] * COLS) >> 5
        rank = jnp.zeros((COLS, DH), jnp.int32)
        for d in range(1, 32 * (R - 1) + PER):
            rank = rank + jnp.where((pltpu.roll(mine, d, 1) == mine) & (lane >= d), 1, 0)
        column = (((mine >> 4) - x) & 3) * NC + (((mine & 1) - c) & 1)
        dy = (((mine >> 1) & 7) - y) & 7
        ring = jnp.where(dy < 4, 2 * dy, jnp.where(dy == 4, 7, 15 - 2 * dy))
        read_v[...] = column * SLOTS + 2 * ring + jnp.minimum(rank, 1)
        t_copies = [
            pltpu.make_async_copy(send_v, send_t, i_s.at[3]),
            pltpu.make_async_copy(read_v, read_t, i_s.at[4]),
        ]
        for copy in t_copies:
            copy.start()
        for copy in t_copies:
            copy.wait()

    y_begin(K0)
    tables()
    x_step(K0, 0)
    edges(K0)
    in_copies[1].wait()
    in_copies[2].wait()
    x_step(V0, 0)
    edges(V0)
    x_step(K1, 0)
    edges(K1)
    y_step(K0, 1)
    y_begin(V0)
    x_step(K0, 1)
    pack()
    w_begin()
    edges(V1A)
    edges(V1B)
    y_step(K0, 2)
    x_step(K0, 2)
    y_step(V0, 1)
    x_step(V0, 1)
    x_step(V1A, 0)
    x_step(V1B, 0)
    y_step(K0, 3)
    x_step(K0, 3)
    y_step(V0, 2)
    x_step(V0, 2)
    w_zeros()
    y_step(K0, 4)
    g_begin(K0)
    x_step(K0, 4)
    y_step(V0, 3)
    y_begin(K1)
    x_step(V0, 3)
    g_mid(K0)
    y_step(V0, 4)
    y_begin(V1A)
    g_begin(V0)
    x_step(V0, 4)
    ready(K0)
    scores(0, 0, 6)
    y_step(K1, 1)
    x_step(K1, 1)
    scores(0, 6, 12)
    g_mid(V0)
    y_step(K1, 2)
    x_step(K1, 2)
    scores(0, 12, 17)
    y_step(V1A, 1)
    x_step(V1A, 1)
    ready(V0)
    context0(0, CUT)
    z_begin(0, 0)
    context0(CUT, PER)
    z_begin(0, 1)
    y_step(K1, 3)
    x_step(K1, 3)
    z_step(0, 1, 0)
    y_step(V1A, 2)
    x_step(V1A, 2)
    z_step(0, 1, 1)
    y_step(K1, 4)
    y_begin(V1B)
    g_begin(K1)
    x_step(K1, 4)
    z_step(0, 2, 0)
    y_step(V1A, 3)
    x_step(V1A, 3)
    z_step(0, 2, 1)
    g_mid(K1)
    y_step(V1A, 4)
    g_begin(V1A)
    x_step(V1A, 4)
    y_step(V1B, 1)
    x_step(V1B, 1)
    z_step(0, 3, 0)
    ready(K1)
    scores(1, 0, 4)
    z_step(0, 3, 1)
    y_step(V1B, 2)
    x_step(V1B, 2)
    g_mid(V1A)
    scores(1, 4, 8)
    y_step(V1B, 3)
    x_step(V1B, 3)
    z_step(0, 4)
    scores(1, 8, 12)
    y_step(V1B, 4)
    g_begin(V1B)
    x_step(V1B, 4)
    scores(1, 12, 17)
    ready(V1A)
    context1(0, 0, CUT)
    z_begin(1, 0)
    context1(0, CUT, PER)
    z_begin(1, 1)
    g_mid(V1B)
    for copy in w_copies:
        copy.wait()
    z_step(1, 1)
    ready(V1B)
    context1(1, 0, CUT)
    z_begin(2, 0)
    z_step(1, 2)
    context1(1, CUT, PER)
    z_begin(2, 1)
    z_step(1, 3)
    project0()
    z_step(1, 4)
    z_step(2, 1)
    project1(0, 0, 8)
    z_step(2, 2)
    project1(1, 0, 5)
    z_step(2, 3)
    project1(1, 5, 7)
    z_step(2, 4)
    project1(1, 7, 8, last=True)

    for copy in pending:
        copy.wait_send()
    for sl in range(5):
        for copy in halo[sl]:
            copy.wait_send()
        x_whole(sl).wait_send()
        g_whole(sl).wait_send()
        g_cores(sl).wait_send()


def on_device(queries, keys, values, rand_group, rand_offset, glob_blocks, w_out):
    n_seq = NX * NY * NC
    code = (rand_group * 32 + rand_offset).T.reshape(R, n_seq, PER)
    code = jnp.pad(code, ((0, 0), (0, 0), (0, DH - PER)), constant_values=-1)
    shape = (PER, BLOCK, HEADS * DH)
    features = w_out.shape[1]
    vmem = pltpu.VMEM

    def per_slice(blocks):
        return [vmem((blocks, height, DH), BF16) for height in HEIGHT]

    scratch = [vmem(shape, BF16)] * 3 + [vmem((COLS, DH), jnp.int32)] * 2 + [pltpu.SMEM((COLS, DH), jnp.int32)] * 2
    scratch += [vmem((PER, height, DH), BF16) for height in HEIGHT for _ in range(NY - 1)]
    for blocks in ((COLS - 1) * SLOTS, COLS * SLOTS, PER + 2, G, 3 * G, G, G, G):
        scratch += per_slice(blocks)
    scratch += [vmem((PER, HALF, DH), BF16)] * 2
    scratch += [vmem((PER, BLOCK, KEYS), BF16)] * 2
    scratch += [vmem((PER, BLOCK, DH), jnp.float32)] * 2
    scratch += [vmem((ROWS, NZ * DH), BF16)] + [vmem((PER * HALF, NZ * DH), BF16)] * 2
    scratch += [vmem((NZ * DH, features), BF16)] * 5
    scratch += [vmem((ROWS, features), jnp.float32)]
    dma = pltpu.SemaphoreType.DMA
    scratch += [dma((5, 16)), dma((5, 16))] + [dma((5,))] * 6 + [dma((5, 2))] * 2
    scratch += [dma((3, 16)), dma((3, 16)), dma((5 * NZ,)), dma((5,))]
    hbm = pl.BlockSpec(memory_space=pl.ANY)
    whole = pl.BlockSpec(memory_space=vmem)
    return pl.pallas_call(
        kernel,
        out_shape=jax.ShapeDtypeStruct((ROWS, features), BF16),
        in_specs=[pl.BlockSpec(memory_space=pltpu.SMEM), whole, hbm, hbm, hbm, hbm],
        out_specs=whole,
        scratch_shapes=scratch,
        compiler_params=pltpu.CompilerParams(collective_id=0, has_side_effects=True, vmem_limit_bytes=60 << 20),
        name="sparse_attention",
    )(glob_blocks, code, queries.reshape(shape), keys.reshape(shape), values.reshape(shape), w_out)


def solution(mesh):
    return jax.shard_map(
        on_device,
        mesh=mesh,
        in_specs=(P("seq", "head"), P("seq", "head"), P("seq", "head"), P(), P(), P(), P(None, "head")),
        out_specs=P("seq", "head"),
        check_vma=False,
    )
```

time: 398 us -> 154 us (0.39)
  waiting for transfers between devices: 282 us -> 0 us
  Pallas kernels: 0 us -> 148 us
  local copies, waits for them, and re-layouts: 48.1 us -> 3.1 us
  starting transfers between devices: 19.6 us -> 0 us
  between operations: 17.3 us -> 0.02 us
  other arithmetic: 17.9 us -> 0.75 us
  matrix products: 11.1 us -> 0 us
    psum x1 -> x0, waiting for transfers between devices: 214 us -> none  [spread(): return lax.psum(block, axis)]
    pallas_call x0 -> x1, Pallas kernels: none -> 148 us  [on_device(): pl.pallas_call(kernel, out_shape=jax.ShapeDtypeStruct((ROWS, features), B...]
    all_gather x1 -> x0, waiting for transfers between devices: 68.1 us -> none  [on_device(): lax.all_gather(context, 'head', axis=1, tiled=True)]
    slice x5 -> x0, local copies, waits for them, and re-layouts: 21.8 us -> none  [the longest x2 14.6 us: attend_sets(): key_part = pair_rows[..., :columns].reshape(block_count, -1, head_count, DH)]
    gather x2 -> x0, local copies, waits for them, and re-layouts: 12.3 us -> none  [the longest x1 6.37 us: on_device(): jnp.take(pair_blocks, send_spot.reshape(-1), axis=0)]
    all_to_all x1 -> x0, starting transfers between devices: 11.6 us -> none  [on_device(): lax.all_to_all(outgoing, 'seq', split_axis=0, concat_axis=0, tiled=True)]
    dot_general x3 -> x0, matrix products: 11.1 us -> none  [the longest x1 5.73 us: on_device(): jnp.dot(lax.all_gather(context, 'head', axis=1, tiled=True), w_out, prefe...]
    select_n x4 -> x0, other arithmetic: 8.16 us -> none  [the longest x1 7.48 us: on_device(): jnp.where(slot_filled[:, :, None, None], outgoing, jnp.zeros_like(outgoing))]
  transfers between devices with their start and end apart: 5 -> 0, of which waited for: 2 -> 0; matrix products, arithmetic and copies ran while one was open for 3% -> 0% of each run, Pallas kernels for 0% -> 0%
where the time goes in v2:
time: 154 us; the launch traced here: 152 us
  Pallas kernels  148 us (96%)
  local copies, waits for them, and re-layouts  3.1 us (2%)
    pallas_call x1, Pallas kernels, on_device(): pl.pallas_call(kernel, out_shape=jax.ShapeDtypeStruct((ROWS, features), B...  148 us

profile of v2, /device:TPU:6, one launch (start us, length us, event | category | flops | bytes accessed | tf_op | source)
XLA Modules:
  0.0 152.2 jit_solution(4193085818712192559)
XLA Ops:
  0.0 0.7 add_bitcast_fusion
  0.7 0.1 reshape.12
  0.9 0.7 pad.4.refs_1_
  1.5 148.3 %sparse_attention.1 = bf16[1088,512]{1,0:T(8,128)(2,1)} custom-call(s32[2]{0:T(128)} %refs_0_.1, s32[3,64,128]{2,1,0:T(8,128)} %pad.4.refs_1_, bf16[17,64,256]{2,1,0:T(8,128)(2,1)} %bitcast.5, bf16[17,64,256]{2,1,0:T(8,128)(2,1)} %bitcast.6, bf16[17,64,256]{2,1,0:T(8,128)(2,1)} %bitcast.7, bf16[2048,512]{1,0:T(8,128)(2,1)} %refs_5_.1), custom_call_target="tpu_custom_call" | custom-call | tf_op jit(solution)/shard_map/sparse_attention/pallas_call | solution.py:536
  149.8 2.3 %copy.9 = bf16[1088,512]{1,0:T(8,128)(2,1)} copy(bf16[1088,512]{1,0:T(8,128)(2,1)} %sparse_attention.1) | data formatting | bytes 2228224

commit v3 on v2

--- a/solution.py
+++ b/solution.py
@@ -10,7 +10,6 @@
 MESH = pl.DeviceIdType.MESH
 DH = 128
 BLOCK = 64
-HALF = 32
 R = 3
 G = 2
 NX, NY, NC, NZ = 4, 8, 2, 8
@@ -25,8 +24,7 @@
 SCALE = 1.0 / math.sqrt(DH)
 STEP_KS = ((0,), (1, 2), (3, 4), (5, 6), (7,))
 Y_OF_K = (0, -1, 1, -2, 2, -3, 3, 4)
-K0, V0, K1, V1A, V1B = range(5)
-HEIGHT = (BLOCK, BLOCK, BLOCK, HALF, HALF)
+K0, V0, K1, V1 = range(4)
 TILE = 272
 BF16 = jnp.bfloat16
 
@@ -39,12 +37,11 @@
 def kernel(*refs):
     glob, code_ref, q_hbm, k_hbm, v_hbm, w_ref, out_ref, *refs = refs
     q_ref, k_ref, v_ref, send_v, read_v, send_t, read_t, *refs = refs
-    y_bufs = [refs[7 * sl : 7 * sl + 7] for sl in range(5)]
-    refs = refs[35:]
-    stage, land, pads, g_out, g_in, g_sel, g_other, g_fin = [refs[5 * n : 5 * n + 5] for n in range(8)]
-    refs = refs[40:]
-    packed, p_bufs, t_bufs, ctx, w_hi, refs = refs[0:2], refs[2:4], refs[4:6], refs[6:9], refs[9:11], refs[11:]
-    w_lo, refs = refs[0:3], refs[3:]
+    y_bufs = [refs[7 * sl : 7 * sl + 7] for sl in range(4)]
+    refs = refs[28:]
+    stage, land, pads, g_out, g_in, g_sel, g_other, g_fin = [refs[4 * n : 4 * n + 4] for n in range(8)]
+    refs = refs[32:]
+    p_bufs, t_bufs, ctx, w_bufs, refs = refs[0:2], refs[2:4], refs[4:6], refs[6:8], refs[8:]
     acc, y_s, y_r, x_s, x_r, g_s, g_r, c_s, c_r, h_s, h_r, z_s, z_r, w_s, i_s = refs
     x, y, c, z = place()
     seq = lax.axis_index("seq")
@@ -77,44 +74,28 @@
 
     w_copies = []
 
-    def w_copy(start, size, dst):
-        copy = pltpu.make_async_copy(w_ref.at[pl.ds(pl.multiple_of(start, HALF), size)], dst, w_s.at[len(w_copies)])
-        copy.start()
-        w_copies.append(copy)
-
     def w_begin():
-        for k in range(NZ):
-            at = (z + Y_OF_K[k] + NZ) % NZ * (HEADS * DH)
-            w_copy(at, DH, w_lo[0].at[pl.ds(k * DH, DH)])
-            for a in range(2):
-                w_copy(at + DH + a * BLOCK, BLOCK, w_lo[1 + a].at[pl.ds(k * DH, BLOCK)])
-                w_copy(at + DH + a * BLOCK, BLOCK, w_hi[a].at[pl.ds(k * DH + BLOCK, BLOCK)])
-
-    def w_zeros():
-        zeros = jnp.zeros((BLOCK, w_ref.shape[1]), BF16)
-        for a in range(2):
+        for h in range(HEADS):
             for k in range(NZ):
-                w_lo[1 + a][pl.ds(k * DH + BLOCK, BLOCK), :] = zeros
-                w_hi[a][pl.ds(k * DH, BLOCK), :] = zeros
+                at = ((z + Y_OF_K[k] + NZ) % NZ * HEADS + h) * DH
+                src = w_ref.at[pl.ds(pl.multiple_of(at, DH), DH)]
+                copy = pltpu.make_async_copy(src, w_bufs[h].at[pl.ds(k * DH, DH)], w_s.at[len(w_copies)])
+                copy.start()
+                w_copies.append(copy)
 
     in_copies[0].wait()
     pl.semaphore_wait(barrier, len(peers))
 
+    def columns(sl):
+        return pl.ds(DH if sl in (K1, V1) else 0, DH)
+
     def source(sl, blocks):
-        if sl in (K0, K1):
-            return k_ref.at[blocks, :, pl.ds(DH if sl == K1 else 0, DH)]
-        if sl == V0:
-            return v_ref.at[blocks, :, pl.ds(0, DH)]
-        return packed[sl - V1A].at[blocks]
+        return (k_ref if sl in (K0, K1) else v_ref).at[blocks, :, columns(sl)]
 
     def load(sl, k, off):
         if k:
             return y_bufs[sl][k - 1][off]
-        if sl in (K0, K1):
-            return k_ref[off, :, pl.ds(DH if sl == K1 else 0, DH)]
-        if sl == V0:
-            return v_ref[off, :, pl.ds(0, DH)]
-        return packed[sl - V1A][off]
+        return (k_ref if sl in (K0, K1) else v_ref)[off, :, columns(sl)]
 
     pending = []
 
@@ -213,7 +194,7 @@
         for g, (_, _, _, c_g) in enumerate(glob_at):
             g_fin[sl][g] = jnp.where(c_g == c, g_sel[sl][g], g_other[sl][g])
 
-    halo = [[] for _ in range(5)]
+    halo = [[] for _ in range(4)]
 
     def edges(sl):
         for n, (src, dst, to) in enumerate(((PER - 1, 0, ahead), (0, PER + 1, behind))):
@@ -232,18 +213,6 @@
             copy.wait_recv()
         x_whole(sl).wait_recv()
         g_end(sl)
-
-    def pack():
-        low = lax.broadcasted_iota(jnp.int32, (HALF, DH), 1) < BLOCK
-
-        def one(i, _):
-            top = v_ref[i, pl.ds(0, HALF), pl.ds(DH, DH)].astype(jnp.float32)
-            bottom = v_ref[i, pl.ds(HALF, HALF), pl.ds(DH, DH)].astype(jnp.float32)
-            packed[0][i] = jnp.where(low, top, pltpu.roll(bottom, BLOCK, 1)).astype(BF16)
-            packed[1][i] = jnp.where(low, pltpu.roll(top, BLOCK, 1), bottom).astype(BF16)
-            return 0
-
-        lax.fori_loop(0, PER, one, 0)
 
     def gathered(sl, i):
         return (
@@ -255,8 +224,6 @@
     def scores(h, begin, end):
         def one(i, _):
             blocks = gathered(K1 if h else K0, i)
-            if h:
-                blocks = [b[:HALF] for b in blocks] + [b[HALF:] for b in blocks]
             s = lax.dot_general(
                 q_ref[i, :, pl.ds(h * DH, DH)],
                 jnp.concatenate(blocks, axis=0),
@@ -271,35 +238,19 @@
 
         lax.fori_loop(begin, end, one, 0)
 
-    def context0(begin, end):
+    def context(h, begin, end):
         def one(i, _):
-            o = jnp.dot(p_bufs[0][i], jnp.concatenate(gathered(V0, i), axis=0), preferred_element_type=jnp.float32)
+            blocks = gathered(V1 if h else V0, i)
+            o = jnp.dot(p_bufs[h][i], jnp.concatenate(blocks, axis=0), preferred_element_type=jnp.float32)
             rows = pl.ds(pl.multiple_of(i * BLOCK, BLOCK), BLOCK)
-            ctx[0][rows, pl.ds(0, DH)] = (o / t_bufs[0][i]).astype(BF16)
+            ctx[h][rows, pl.ds(0, DH)] = (o / t_bufs[h][i]).astype(BF16)
             return 0
 
         lax.fori_loop(begin, end, one, 0)
 
-    def context1(a, begin, end):
-        low = lax.broadcasted_iota(jnp.int32, (HALF, DH), 1) < BLOCK
-        half_keys = KEYS // 2
-
-        def one(i, _):
-            p = jnp.concatenate([p_bufs[1][i, :, pl.ds(0, half_keys)], p_bufs[1][i, :, pl.ds(half_keys, half_keys)]])
-            o = jnp.dot(p, jnp.concatenate(gathered(V1A + a, i), axis=0), preferred_element_type=jnp.float32)
-            upper = o[0:HALF] + pltpu.roll(o[BLOCK : BLOCK + HALF], BLOCK, 1)
-            lower = pltpu.roll(o[HALF:BLOCK], BLOCK, 1) + o[BLOCK + HALF :]
-            total = jnp.where(low, t_bufs[1][i, pl.ds(0, HALF)], t_bufs[1][i, pl.ds(HALF, HALF)])
-            rows = pl.ds(pl.multiple_of(i * HALF, HALF), HALF)
-            ctx[1 + a][rows, pl.ds(0, DH)] = (jnp.where(low, upper, lower) / total).astype(BF16)
-            return 0
-
-        lax.fori_loop(begin, end, one, 0)
-
     def z_copy(t, step, up, piece):
-        height = HALF if t else BLOCK
         first, size = PIECES[piece]
-        rows = pl.ds(first * height, size * height)
+        rows = pl.ds(first * BLOCK, size * BLOCK)
         from_k = 0 if step == 1 else 2 * step - (3 if up else 2)
         to_k = 7 if step == 4 else 2 * step - (1 if up else 0)
         n = (step - 1) * 4 + (0 if up else 2) + piece
@@ -323,27 +274,21 @@
             if (piece, up) in moves(step + 1):
                 start(z_copy(t, step + 1, up, piece))
 
-    def project0():
+    def project(h, k0, k1, begin=0, end=ROWS // TILE, first=False, last=False):
+        cols = pl.ds(k0 * DH, (k1 - k0) * DH)
+
         def tile(n, _):
             rows = pl.ds(pl.multiple_of(n * TILE, 16), TILE)
-            acc[rows, :] = jnp.dot(ctx[0][rows, :], w_lo[0][...], preferred_element_type=jnp.float32)
+            part = jnp.dot(ctx[h][rows, cols], w_bufs[h][cols, :], preferred_element_type=jnp.float32)
+            if not first:
+                part = part + acc[rows, :]
+            if last:
+                out_ref[rows, :] = part.astype(out_ref.dtype)
+            else:
+                acc[rows, :] = part
             return 0
 
-        lax.fori_loop(0, ROWS // TILE, tile, 0)
-
-    def project1(a, k0, k1, last=False):
-        cols = pl.ds(k0 * DH, (k1 - k0) * DH)
-        for b0, b1 in ((0, 6), (6, 12), (12, PER)):
-            lhs = ctx[1 + a][pl.ds(b0 * HALF, (b1 - b0) * HALF), cols]
-            for w, shift in ((w_lo[1 + a], 0), (w_hi[a], HALF)):
-                part = jnp.dot(lhs, w[cols, :], preferred_element_type=jnp.float32)
-                for b in range(b0, b1):
-                    rows = pl.ds(b * BLOCK + shift, HALF)
-                    total = acc[rows, :] + part[(b - b0) * HALF : (b - b0 + 1) * HALF]
-                    if last:
-                        out_ref[rows, :] = total.astype(out_ref.dtype)
-                    else:
-                        acc[rows, :] = total
+        lax.fori_loop(begin, end, tile, 0)
 
     def tables():
         lane = lax.broadcasted_iota(jnp.int32, (COLS, DH), 1)
@@ -390,116 +335,90 @@
     x_step(K1, 0)
     edges(K1)
     y_step(K0, 1)
+    x_step(K0, 1)
+    w_begin()
+    edges(V1)
+    y_step(K0, 2)
     y_begin(V0)
-    x_step(K0, 1)
-    pack()
-    w_begin()
-    edges(V1A)
-    edges(V1B)
-    y_step(K0, 2)
     x_step(K0, 2)
+    x_step(V1, 0)
+    y_step(K0, 3)
+    x_step(K0, 3)
     y_step(V0, 1)
     x_step(V0, 1)
-    x_step(V1A, 0)
-    x_step(V1B, 0)
-    y_step(K0, 3)
-    x_step(K0, 3)
-    y_step(V0, 2)
-    x_step(V0, 2)
-    w_zeros()
     y_step(K0, 4)
     g_begin(K0)
     x_step(K0, 4)
+    y_step(V0, 2)
+    y_begin(K1)
+    x_step(V0, 2)
+    g_mid(K0)
     y_step(V0, 3)
-    y_begin(K1)
     x_step(V0, 3)
-    g_mid(K0)
+    ready(K0)
+    scores(0, 0, 5)
+    y_step(K1, 1)
+    x_step(K1, 1)
+    scores(0, 5, 9)
     y_step(V0, 4)
-    y_begin(V1A)
     g_begin(V0)
     x_step(V0, 4)
-    ready(K0)
-    scores(0, 0, 6)
-    y_step(K1, 1)
-    x_step(K1, 1)
-    scores(0, 6, 12)
+    scores(0, 9, 13)
+    y_step(K1, 2)
+    y_begin(V1)
+    x_step(K1, 2)
+    scores(0, 13, 17)
     g_mid(V0)
-    y_step(K1, 2)
-    x_step(K1, 2)
-    scores(0, 12, 17)
-    y_step(V1A, 1)
-    x_step(V1A, 1)
-    ready(V0)
-    context0(0, CUT)
-    z_begin(0, 0)
-    context0(CUT, PER)
-    z_begin(0, 1)
     y_step(K1, 3)
     x_step(K1, 3)
-    z_step(0, 1, 0)
-    y_step(V1A, 2)
-    x_step(V1A, 2)
-    z_step(0, 1, 1)
+    ready(V0)
+    context(0, 0, CUT)
+    z_begin(0, 0)
+    context(0, CUT, PER)
+    z_begin(0, 1)
+    y_step(V1, 1)
+    x_step(V1, 1)
     y_step(K1, 4)
-    y_begin(V1B)
     g_begin(K1)
     x_step(K1, 4)
-    z_step(0, 2, 0)
-    y_step(V1A, 3)
-    x_step(V1A, 3)
-    z_step(0, 2, 1)
+    z_step(0, 1)
+    y_step(V1, 2)
+    x_step(V1, 2)
     g_mid(K1)
-    y_step(V1A, 4)
-    g_begin(V1A)
-    x_step(V1A, 4)
-    y_step(V1B, 1)
-    x_step(V1B, 1)
-    z_step(0, 3, 0)
+    z_step(0, 2)
+    y_step(V1, 3)
+    x_step(V1, 3)
     ready(K1)
-    scores(1, 0, 4)
-    z_step(0, 3, 1)
-    y_step(V1B, 2)
-    x_step(V1B, 2)
-    g_mid(V1A)
-    scores(1, 4, 8)
-    y_step(V1B, 3)
-    x_step(V1B, 3)
+    scores(1, 0, 5)
+    z_step(0, 3)
+    y_step(V1, 4)
+    g_begin(V1)
+    x_step(V1, 4)
+    scores(1, 5, 11)
+    g_mid(V1)
+    scores(1, 11, 17)
     z_step(0, 4)
-    scores(1, 8, 12)
-    y_step(V1B, 4)
-    g_begin(V1B)
-    x_step(V1B, 4)
-    scores(1, 12, 17)
-    ready(V1A)
-    context1(0, 0, CUT)
-    z_begin(1, 0)
-    context1(0, CUT, PER)
-    z_begin(1, 1)
-    g_mid(V1B)
     for copy in w_copies:
         copy.wait()
-    z_step(1, 1)
-    ready(V1B)
-    context1(1, 0, CUT)
-    z_begin(2, 0)
+    ready(V1)
+    context(1, 0, CUT)
+    z_begin(1, 0)
+    context(1, CUT, PER)
+    z_begin(1, 1)
+    project(0, 0, 8, 0, 2, first=True)
+    z_step(1, 1, 0)
+    z_step(1, 1, 1)
+    project(0, 0, 8, 2, 4, first=True)
     z_step(1, 2)
-    context1(1, CUT, PER)
-    z_begin(2, 1)
+    project(1, 0, 5)
     z_step(1, 3)
-    project0()
+    project(1, 5, 7)
     z_step(1, 4)
-    z_step(2, 1)
-    project1(0, 0, 8)
-    z_step(2, 2)
-    project1(1, 0, 5)
-    z_step(2, 3)
-    project1(1, 5, 7)
-    z_step(2, 4)
-    project1(1, 7, 8, last=True)
+    project(1, 7, 8, last=True)
 
     for copy in pending:
         copy.wait_send()
-    for sl in range(5):
+    for sl in range(4):
         for copy in halo[sl]:
             copy.wait_send()
         x_whole(sl).wait_send()
@@ -516,21 +435,20 @@
     vmem = pltpu.VMEM
 
     def per_slice(blocks):
-        return [vmem((blocks, height, DH), BF16) for height in HEIGHT]
+        return [vmem((blocks, BLOCK, DH), BF16)] * 4
 
     scratch = [vmem(shape, BF16)] * 3 + [vmem((COLS, DH), jnp.int32)] * 2 + [pltpu.SMEM((COLS, DH), jnp.int32)] * 2
-    scratch += [vmem((PER, height, DH), BF16) for height in HEIGHT for _ in range(NY - 1)]
+    scratch += per_slice(PER) * (NY - 1)
     for blocks in ((COLS - 1) * SLOTS, COLS * SLOTS, PER + 2, G, 3 * G, G, G, G):
         scratch += per_slice(blocks)
-    scratch += [vmem((PER, HALF, DH), BF16)] * 2
     scratch += [vmem((PER, BLOCK, KEYS), BF16)] * 2
     scratch += [vmem((PER, BLOCK, DH), jnp.float32)] * 2
-    scratch += [vmem((ROWS, NZ * DH), BF16)] + [vmem((PER * HALF, NZ * DH), BF16)] * 2
-    scratch += [vmem((NZ * DH, features), BF16)] * 5
+    scratch += [vmem((ROWS, NZ * DH), BF16)] * 2
+    scratch += [vmem((NZ * DH, features), BF16)] * 2
     scratch += [vmem((ROWS, features), jnp.float32)]
     dma = pltpu.SemaphoreType.DMA
-    scratch += [dma((5, 16)), dma((5, 16))] + [dma((5,))] * 6 + [dma((5, 2))] * 2
-    scratch += [dma((3, 16)), dma((3, 16)), dma((5 * NZ,)), dma((5,))]
+    scratch += [dma((4, 16)), dma((4, 16))] + [dma((4,))] * 6 + [dma((4, 2))] * 2
+    scratch += [dma((2, 16)), dma((2, 16)), dma((HEADS * NZ,)), dma((5,))]
     hbm = pl.BlockSpec(memory_space=pl.ANY)
     whole = pl.BlockSpec(memory_space=vmem)
     return pl.pallas_call(

time: 154 us -> 146 us (0.948)
  Pallas kernels: 148 us -> 141 us
    pallas_call x1, Pallas kernels: 148 us -> 141 us  [on_device(): pl.pallas_call(kernel, out_shape=jax.ShapeDtypeStruct((ROWS, features), B...]
where the time goes in v3:
time: 146 us; the launch traced here: 145 us
  Pallas kernels  141 us (97%)
  local copies, waits for them, and re-layouts  3.1 us (2%)
    pallas_call x1, Pallas kernels, on_device(): pl.pallas_call(kernel, out_shape=jax.ShapeDtypeStruct((ROWS, features), B...  141 us

profile of v3, /device:TPU:6, one launch (start us, length us, event | category | flops | bytes accessed | tf_op | source)
XLA Modules:
  0.0 145.1 jit_solution(14118003693856638981)
XLA Ops:
  0.0 0.7 add_bitcast_fusion
  0.7 0.1 reshape.12
  0.9 0.7 pad.4.refs_1_
  1.5 141.3 %sparse_attention.1 = bf16[1088,512]{1,0:T(8,128)(2,1)} custom-call(s32[2]{0:T(128)} %refs_0_.1, s32[3,64,128]{2,1,0:T(8,128)} %pad.4.refs_1_, bf16[17,64,256]{2,1,0:T(8,128)(2,1)} %bitcast.5, bf16[17,64,256]{2,1,0:T(8,128)(2,1)} %bitcast.6, bf16[17,64,256]{2,1,0:T(8,128)(2,1)} %bitcast.7, bf16[2048,512]{1,0:T(8,128)(2,1)} %refs_5_.1), custom_call_target="tpu_custom_call" | custom-call | tf_op jit(solution)/shard_map/sparse_attention/pallas_call | solution.py:454
  142.8 2.3 %copy.9 = bf16[1088,512]{1,0:T(8,128)(2,1)} copy(bf16[1088,512]{1,0:T(8,128)(2,1)} %sparse_attention.1) | data formatting | bytes 2228224

commit v4 on v3

--- a/solution.py
+++ b/solution.py
@@ -21,6 +21,7 @@
 KEYS = 8 * BLOCK
 CUT = 9
 PIECES = ((0, CUT), (CUT, PER - CUT))
+LAST_PIECES = ((0, 5), (5, 4), (9, 4), (13, 4))
 SCALE = 1.0 / math.sqrt(DH)
 STEP_KS = ((0,), (1, 2), (3, 4), (5, 6), (7,))
 Y_OF_K = (0, -1, 1, -2, 2, -3, 3, 4)
@@ -113,8 +114,9 @@
         n = (step - 1) * 4 + (0 if up else 2) + piece
         return remote(src, dst, y_s.at[sl, n], y_r.at[sl, n], y_up if up else y_down)
 
-    def moves(step):
-        return [(piece, up) for piece in (0, 1) for up in (True, False) if step < 4 or (step == 4 and up == (piece == 0))]
+    def moves(step, count=2):
+        both = [(piece, up) for piece in range(count) for up in (True, False)]
+        return both if step < 4 else [(piece, up) for piece, up in both if step == 4 and up == (2 * piece < count)]
 
     def y_begin(sl):
         for piece, up in moves(1):
@@ -249,11 +251,12 @@
         lax.fori_loop(begin, end, one, 0)
 
     def z_copy(t, step, up, piece):
-        first, size = PIECES[piece]
+        pieces = LAST_PIECES if t else PIECES
+        first, size = pieces[piece]
         rows = pl.ds(first * BLOCK, size * BLOCK)
         from_k = 0 if step == 1 else 2 * step - (3 if up else 2)
         to_k = 7 if step == 4 else 2 * step - (1 if up else 0)
-        n = (step - 1) * 4 + (0 if up else 2) + piece
+        n = (step - 1) * 8 + (0 if up else 4) + piece
         return remote(
             ctx[t].at[rows, pl.ds(from_k * DH, DH)],
             ctx[t].at[rows, pl.ds(to_k * DH, DH)],
@@ -267,11 +270,12 @@
             start(z_copy(t, 1, up, piece))
 
     def z_step(t, step, only=None):
-        for piece, up in moves(step):
-            if only is not None and piece != only:
+        count = len(LAST_PIECES if t else PIECES)
+        for piece, up in moves(step, count):
+            if only is not None and piece not in only:
                 continue
             z_copy(t, step, up, piece).wait_recv()
-            if (piece, up) in moves(step + 1):
+            if (piece, up) in moves(step + 1, count):
                 start(z_copy(t, step + 1, up, piece))
 
     def project(h, k0, k1, begin=0, end=ROWS // TILE, first=False, last=False):
@@ -401,17 +405,17 @@
     for copy in w_copies:
         copy.wait()
     ready(V1)
-    context(1, 0, CUT)
-    z_begin(1, 0)
-    context(1, CUT, PER)
-    z_begin(1, 1)
+    for piece, (first, size) in enumerate(LAST_PIECES):
+        context(1, first, first + size)
+        z_begin(1, piece)
     project(0, 0, 8, 0, 2, first=True)
-    z_step(1, 1, 0)
-    z_step(1, 1, 1)
+    z_step(1, 1)
     project(0, 0, 8, 2, 4, first=True)
     z_step(1, 2)
-    project(1, 0, 5)
-    z_step(1, 3)
+    project(1, 0, 5, 0, 2)
+    z_step(1, 3, (0, 1))
+    project(1, 0, 5, 2, 4)
+    z_step(1, 3, (2, 3))
     project(1, 5, 7)
     z_step(1, 4)
     project(1, 7, 8, last=True)
@@ -448,7 +452,7 @@
     scratch += [vmem((ROWS, features), jnp.float32)]
     dma = pltpu.SemaphoreType.DMA
     scratch += [dma((4, 16)), dma((4, 16))] + [dma((4,))] * 6 + [dma((4, 2))] * 2
-    scratch += [dma((2, 16)), dma((2, 16)), dma((HEADS * NZ,)), dma((5,))]
+    scratch += [dma((2, 32)), dma((2, 32)), dma((HEADS * NZ,)), dma((5,))]
     hbm = pl.BlockSpec(memory_space=pl.ANY)
     whole = pl.BlockSpec(memory_space=vmem)
     return pl.pallas_call(

time: 146 us -> 146 us (level)
  no operation moved by 1% of the time
where the time goes in v4:
time: 146 us; the launch traced here: 145 us
  Pallas kernels  141 us (97%)
  local copies, waits for them, and re-layouts  3.1 us (2%)
    pallas_call x1, Pallas kernels, on_device(): pl.pallas_call(kernel, out_shape=jax.ShapeDtypeStruct((ROWS, features), B...  141 us

profile of v4, /device:TPU:6, one launch (start us, length us, event | category | flops | bytes accessed | tf_op | source)
XLA Modules:
  0.0 145.1 jit_solution(11933391934732824684)
XLA Ops:
  0.0 0.7 add_bitcast_fusion
  0.7 0.1 reshape.12
  0.9 0.7 pad.4.refs_1_
  1.5 141.2 %sparse_attention.1 = bf16[1088,512]{1,0:T(8,128)(2,1)} custom-call(s32[2]{0:T(128)} %refs_0_.1, s32[3,64,128]{2,1,0:T(8,128)} %pad.4.refs_1_, bf16[17,64,256]{2,1,0:T(8,128)(2,1)} %bitcast.5, bf16[17,64,256]{2,1,0:T(8,128)(2,1)} %bitcast.6, bf16[17,64,256]{2,1,0:T(8,128)(2,1)} %bitcast.7, bf16[2048,512]{1,0:T(8,128)(2,1)} %refs_5_.1), custom_call_target="tpu_custom_call" | custom-call | tf_op jit(solution)/shard_map/sparse_attention/pallas_call | solution.py:458
  142.8 2.3 %copy.9 = bf16[1088,512]{1,0:T(8,128)(2,1)} copy(bf16[1088,512]{1,0:T(8,128)(2,1)} %sparse_attention.1) | data formatting | bytes 2228224
